TPU v7x, 32 devices: a whole 2x2x4 slice. The times are simulated.
32 devices in a mesh: grp: 2 (over x), seq: 16 (over z, y, core).
Axes of the slice: x: 2, y: 2, z: 4, core: 2. Of those that a mesh axis runs over, the one named last changes fastest.
Arguments:
- queries: bfloat16 [4096, 8192], P(('grp', 'seq')), parts along dimension 0, may hold values from -8 to 8, as said below
- new_kv: bfloat16 [4096, 2048], P(('grp', 'seq')), parts along dimension 0, may hold values from -6 to 6
- cache: bfloat16 [32, 8192, 256], P(('grp', 'seq')), parts along dimension 0, may hold values from -4 to 4, as said below
- tile_lists: int32 [128, 16, 8], P(('grp', 'seq')), parts along dimension 0, may hold values from 0 to 63, as said below
- tile_counts: int32 [128, 16], P(('grp', 'seq')), parts along dimension 0, may hold values from 1 to 8, as said below
- tile_mask: int32 [32, 16], P('grp'), parts along dimension 0, may hold values from 0 to 1, as said below
Outputs:
- attended: bfloat16 [4096, 8192], P(('grp', 'seq')), parts along dimension 0
There are 2 independent parts, one for each index of `grp`. A program takes and returns all parts, laid end to end along the dimension named above; each array names one. Nothing has to cross between parts.
Inputs may be any that keep to these rules, and one draw needn't show every extreme that they name: `queries`: row t, query head h: positions and heads laid out as stated; values within the range. cache[d] is the cache of kv head d * 8 // 16; the 2 copies of one kv head are equal. `tile_lists`: the valid slots of a list name different cache tiles; slots past the count hold tile numbers that are not attended. `tile_counts`: some list of some head has all 8 slots valid. `tile_mask`: the diagonal is 1, every entry above it is 0, and entry (i, j) is 0 wherever j // 4 < i // 4 - 3.
All inputs are finite; a program needn't handle non-finite values.
Results may differ from a plain program's by a relative error of at most 0.0065.
Values may be sent and summed in bfloat16 or wider, within the bound.
A program may use at most 128 MiB of HBM per device.

v0:
```python
import functools
import math

import jax
import jax.numpy as jnp
from jax import lax
from jax.experimental import pallas as pl
from jax.experimental.pallas import tpu as pltpu
from jax.sharding import PartitionSpec as P

TILE = 128
REACH = 3
GROUP = 4
MESH = pl.DeviceIdType.MESH
NEG = -jnp.inf


def dot_t(a, b):
    return lax.dot_general(a, b, (((1,), (1,)), ((), ())), preferred_element_type=jnp.float32)


def keep_if(value, above, part):
    return jnp.where(jnp.full(part.shape, value, jnp.int32) > above, part, NEG)


def attend_block(h, b, slots, qbuf, kvbuf, cbuf, lists, counts, mask, scores, peaks, accum, obuf):
    hd = qbuf.shape[-1]
    rows = GROUP * TILE
    scale = math.log2(math.e) / math.sqrt(hd)
    base = pl.multiple_of(b * rows, rows)
    first = jnp.maximum(b - REACH, 0)
    span_at = slots * TILE

    def cache_scores(t, _):
        tile = b * GROUP + t
        count = counts[h, tile]
        start = pl.multiple_of(base + t * TILE, TILE)
        here = pl.ds(pl.multiple_of(t * TILE, TILE), TILE)
        q = qbuf[h, pl.ds(start, TILE), :]
        top = None
        for j in range(0, slots, 2):
            keys = jnp.concatenate(
                [cbuf[lists[h, j + k, tile], :, :hd] for k in range(2)], axis=0
            )
            s = dot_t(q, keys)
            for k in range(2):
                part = keep_if(count, j + k, s[:, k * TILE : (k + 1) * TILE])
                scores[here, (j + k) * TILE : (j + k + 1) * TILE] = part
                top = part if top is None else jnp.maximum(top, part)
        peaks[here, :] = top
        return 0

    lax.fori_loop(0, GROUP, cache_scores, 0, unroll=True)

    def span_scores(kb, diagonal):
        q = qbuf[h, pl.ds(base, rows), :]
        col = pl.multiple_of(span_at + (kb - first) * rows, rows)
        if diagonal:
            lower = lax.broadcasted_iota(jnp.int32, (TILE, TILE), 1) <= lax.broadcasted_iota(
                jnp.int32, (TILE, TILE), 0
            )
        for half in range(2):
            keys = kvbuf[kb * 2 + half, :, :, :hd].reshape(2 * TILE, hd)
            s = dot_t(q, keys)
            for t in range(GROUP):
                top = peaks[t * TILE : (t + 1) * TILE, :]
                for k in range(2):
                    u = half * 2 + k
                    part = s[t * TILE : (t + 1) * TILE, k * TILE : (k + 1) * TILE]
                    if diagonal and u > t:
                        part = jnp.full((TILE, TILE), NEG, jnp.float32)
                    else:
                        if diagonal and u == t:
                            part = jnp.where(lower, part, NEG)
                        part = keep_if(mask[b * GROUP + t, kb * GROUP + u], 0, part)
                        top = jnp.maximum(top, part)
                    scores[t * TILE : (t + 1) * TILE, pl.ds(col + u * TILE, TILE)] = part
                peaks[t * TILE : (t + 1) * TILE, :] = top

    def off_diagonal(kb, _):
        span_scores(kb, False)
        return 0

    lax.fori_loop(first, b, off_diagonal, 0)
    span_scores(b, True)

    def cache_mix(t, _):
        tile = b * GROUP + t
        here = pl.ds(pl.multiple_of(t * TILE, TILE), TILE)
        peak = jnp.max(peaks[here, :], axis=1, keepdims=True)
        peak = jnp.broadcast_to(peak, (TILE, TILE))
        peaks[here, :] = peak
        ones = jnp.ones((TILE, hd), jnp.bfloat16)
        total = None
        for j in range(0, slots, 2):
            values = jnp.concatenate(
                [
                    jnp.concatenate([cbuf[lists[h, j + k, tile], :, hd:], ones], axis=1)
                    for k in range(2)
                ],
                axis=0,
            )
            weights = jnp.concatenate(
                [
                    jnp.exp2(
                        (scores[here, (j + k) * TILE : (j + k + 1) * TILE] - peak) * scale
                    ).astype(jnp.bfloat16)
                    for k in range(2)
                ],
                axis=1,
            )
            mixed = jnp.dot(weights, values, preferred_element_type=jnp.float32)
            total = mixed if total is None else total + mixed
        accum[here, :] = total
        return 0

    lax.fori_loop(0, GROUP, cache_mix, 0, unroll=True)

    def span_mix(kb, _):
        col = pl.multiple_of(span_at + (kb - first) * rows, rows)
        ones = jnp.ones((rows, hd), jnp.bfloat16)
        values = kvbuf[pl.ds(kb * 2, 2), :, :, hd:].reshape(rows, hd)
        values = jnp.concatenate([values, ones], axis=1)
        for t in range(GROUP):
            here = slice(t * TILE, (t + 1) * TILE)
            peak = peaks[here, :]
            weights = jnp.concatenate(
                [
                    jnp.exp2(
                        (scores[here, pl.ds(col + u * TILE, TILE)] - peak) * scale
                    ).astype(jnp.bfloat16)
                    for u in range(GROUP)
                ],
                axis=1,
            )
            accum[here, :] += jnp.dot(weights, values, preferred_element_type=jnp.float32)
        return 0

    lax.fori_loop(first, b + 1, span_mix, 0)
    obuf[h, pl.ds(base, rows), :] = (accum[:, :hd] / accum[:, hd:]).astype(jnp.bfloat16)


def fused(
    n, kv_heads, slots,
    lists_ref, counts_ref, mask_ref, q_ref, kv_ref, c_ref, out_ref,
    lists, counts, mask, qbuf, kvbuf, cbuf, obuf, scores, peaks, accum,
    s_sem, c_sem, l_sem, kv_send, kv_recv, f_send, f_recv, q_send, q_recv, o_send, o_recv,
):
    me = lax.axis_index("seq")
    heads, _, hd = qbuf.shape
    chips = n // 2
    core = lax.rem(me, 2)
    sibling = me + 1 - 2 * core
    my_chip = me // 2

    blocks = n // GROUP
    half = blocks // 2

    def far_first(step):
        z = me // GROUP
        upper = lax.rem(z // half + 1 + step // half, 2)
        return upper * half + lax.rem(z + 1 + step, half)

    cache_copy = pltpu.make_async_copy(c_ref, cbuf, c_sem)
    cache_copy.start()

    small = [
        pltpu.make_async_copy(src, dst, s_sem.at[k])
        for k, (src, dst) in enumerate(((lists_ref, lists), (counts_ref, counts), (mask_ref, mask)))
    ]
    for copy in small:
        copy.start()
    barrier = pltpu.get_barrier_semaphore()

    def greet(k, _):
        pl.semaphore_signal(barrier, inc=1, device_id={"seq": lax.rem(me + k, n)}, device_id_type=MESH)
        return 0

    lax.fori_loop(1, n, greet, 0)

    def own_q(h):
        return pltpu.make_async_copy(
            q_ref.at[:, pl.ds(pl.multiple_of((me * heads + h) * hd, hd), hd)],
            qbuf.at[h, pl.ds(pl.multiple_of(me * TILE, TILE), TILE), :],
            l_sem.at[h],
        )

    def kv_cols(chip):
        return pl.ds(pl.multiple_of((2 * chip * kv_heads // n) * 2 * hd, 2 * hd), 2 * hd)

    own_kv = pltpu.make_async_copy(kv_ref.at[:, kv_cols(my_chip)], kvbuf.at[my_chip, core], l_sem.at[heads])
    own_kv.start()
    for h in range(heads):
        own_q(h).start()
    pl.semaphore_wait(barrier, n - 1)

    def send_kv(k, _):
        chip = lax.rem(my_chip + chips // 2 + k, chips)

        @pl.when(chip != my_chip)
        def _():
            pltpu.make_async_remote_copy(
                src_ref=kv_ref.at[:, kv_cols(chip)],
                dst_ref=kvbuf.at[my_chip, core],
                send_sem=kv_send,
                recv_sem=kv_recv,
                device_id={"seq": 2 * chip + core},
                device_id_type=MESH,
            ).start()

        return 0

    lax.fori_loop(0, chips, send_kv, 0)

    def send_q(step, _):
        h = step // n
        turn = lax.rem(step, n)
        peer = far_first(turn // GROUP) * GROUP + lax.rem(me + turn, GROUP)

        @pl.when(peer != me)
        def _():
            pltpu.make_async_remote_copy(
                src_ref=q_ref.at[:, pl.ds(pl.multiple_of((peer * heads + h) * hd, hd), hd)],
                dst_ref=qbuf.at[h, pl.ds(pl.multiple_of(me * TILE, TILE), TILE), :],
                send_sem=q_send,
                recv_sem=q_recv.at[h],
                device_id={"seq": peer},
                device_id_type=MESH,
            ).start()

        return 0

    lax.fori_loop(0, heads * n, send_q, 0)

    def take(ref, sem):
        pltpu.make_async_copy(ref, ref, sem).wait()

    own_kv.wait()
    take(kvbuf.at[pl.ds(0, chips - 1), 0], kv_recv)
    forward = pltpu.make_async_remote_copy(
        src_ref=kvbuf.at[:, core],
        dst_ref=kvbuf.at[:, core],
        send_sem=f_send,
        recv_sem=f_recv,
        device_id={"seq": sibling},
        device_id_type=MESH,
    )
    forward.start()
    cache_copy.wait()
    for copy in small:
        copy.wait()
    forward.wait()

    def one_head(h, _):
        own_q(h).wait()
        take(qbuf.at[h, pl.ds(0, (n - 1) * TILE), :], q_recv.at[h])

        def one_block(step, _):
            b = far_first(step)
            attend_block(
                h, b, slots, qbuf, kvbuf, cbuf, lists, counts, mask, scores, peaks, accum, obuf
            )
            cols = pl.ds(pl.multiple_of((me * heads + h) * hd, hd), hd)
            for t in range(GROUP):
                peer = b * GROUP + t
                src = obuf.at[h, pl.ds(pl.multiple_of(peer * TILE, TILE), TILE), :]

                @pl.when(peer != me)
                def _():
                    pltpu.make_async_remote_copy(
                        src_ref=src,
                        dst_ref=out_ref.at[:, cols],
                        send_sem=o_send,
                        recv_sem=o_recv,
                        device_id={"seq": peer},
                        device_id_type=MESH,
                    ).start()

                @pl.when(peer == me)
                def _():
                    pltpu.make_async_copy(src, out_ref.at[:, cols], l_sem.at[heads + 1]).start()

            return 0

        lax.fori_loop(0, blocks, one_block, 0)
        return 0

    lax.fori_loop(0, heads, one_head, 0)

    wide = pl.ds(0, (n - 1) * heads * hd)
    take(kvbuf.at[pl.ds(0, chips - 1), 0], kv_send)
    take(q_ref.at[:, wide], q_send)
    take(q_ref.at[:, wide], o_send)
    take(out_ref.at[:, wide], o_recv)
    take(out_ref.at[:, pl.ds(0, heads * hd)], l_sem.at[heads + 1])


def per_device(queries, new_kv, cache, tile_lists, tile_counts, tile_mask):
    n = lax.axis_size("seq")
    hd = cache.shape[2] // 2
    kv_heads = new_kv.shape[1] // (2 * hd)
    heads, tiles, slots = tile_lists.shape
    tokens = tiles * TILE
    rows = GROUP * TILE
    reach = min(REACH + 1, tiles // GROUP)
    bf, f32 = jnp.bfloat16, jnp.float32
    dma = pltpu.SemaphoreType.DMA
    hbm = pl.BlockSpec(memory_space=pl.ANY)
    return pl.pallas_call(
        functools.partial(fused, n, kv_heads, slots),
        out_shape=pltpu.VMEM(queries.shape, bf),
        in_specs=[hbm] * 6,
        out_specs=hbm,
        scratch_shapes=[
            pltpu.SMEM((heads, slots, tiles), jnp.int32),
            pltpu.SMEM((heads, tiles), jnp.int32),
            pltpu.SMEM(tile_mask.shape, jnp.int32),
            pltpu.VMEM((heads, tokens, hd), bf),
            pltpu.VMEM((n // 2, 2, TILE, 2 * hd), bf),
            pltpu.VMEM((cache.shape[1] // TILE, TILE, 2 * hd), bf),
            pltpu.VMEM((heads, tokens, hd), bf),
            pltpu.VMEM((rows, slots * TILE + reach * rows), f32),
            pltpu.VMEM((rows, TILE), f32),
            pltpu.VMEM((rows, 2 * hd), f32),
            dma((3,)), dma, dma((heads + 2,)), dma, dma, dma, dma, dma, dma((heads,)), dma, dma,
        ],
        compiler_params=pltpu.CompilerParams(
            collective_id=0, has_side_effects=True, vmem_limit_bytes=60 * 1024 * 1024
        ),
    )(tile_lists.transpose(0, 2, 1), tile_counts, tile_mask, queries, new_kv, cache.reshape(-1, TILE, 2 * hd))


def solution(mesh):
    placed = (
        P(("grp", "seq"), None),
        P(("grp", "seq"), None),
        P(("grp", "seq"), None, None),
        P(("grp", "seq"), None, None),
        P(("grp", "seq"), None),
        P("grp", None),
    )
    return jax.shard_map(
        per_device, mesh=mesh, in_specs=placed, out_specs=P(("grp", "seq"), None), check_vma=False
    )
```

profile of v0, /device:TPU:5, one launch (start us, length us, event | category | flops | bytes accessed | tf_op | source)
XLA Modules:
  0.0 109.1 jit_solution(8596689495831940064)
XLA Ops:
  0.0 107.8 %shard_map.64 = bf16[128,8192]{1,0:T(8,128)(2,1)S(1)} custom-call(s32[4,8,16]{2,1,0:T(8,128)} %bitcast.3, s32[4,16]{1,0:T(4,128)} %counts_ref.1, s32[16,16]{1,0:T(8,128)} %mask_ref.1, bf16[128,8192]{1,0:T(8,128)(2,1)} %q_ref.1, bf16[128,2048]{1,0:T(8,128)(2,1)} %kv_ref.1, bf16[64,128,256]{2,1,0:T(8,128)(2,1)} %bitcast.2), custom_call_target="tpu_custom_call" | custom-call | tf_op jit(solution)/shard_map/pallas_call | solution.py:309
  107.8 1.3 %copy.8 = bf16[128,8192]{1,0:T(8,128)(2,1)} copy(bf16[128,8192]{1,0:T(8,128)(2,1)S(1)} %shard_map.64) | data formatting | bytes 4194304
where the time goes:
time: 109 us
  Pallas kernels  108 us (99%)
  local copies, waits for them, and re-layouts  1.32 us (1%)
    pallas_call x1, Pallas kernels, per_device(): pl.pallas_call(functools.partial(fused, n, kv_heads, slots), out_shape=pl...  108 us

commit v1 on v0

--- a/solution.py
+++ b/solution.py
@@ -144,7 +144,7 @@
     n, kv_heads, slots,
     lists_ref, counts_ref, mask_ref, q_ref, kv_ref, c_ref, out_ref,
     lists, counts, mask, qbuf, kvbuf, cbuf, obuf, scores, peaks, accum,
-    s_sem, c_sem, l_sem, kv_send, kv_recv, f_send, f_recv, q_send, q_recv, o_send, o_recv,
+    above_sem, below_sem, s_sem, c_sem, l_sem, kv_send, kv_recv, f_send, f_recv, q_send, q_recv, o_send, o_recv,
 ):
     me = lax.axis_index("seq")
     heads, _, hd = qbuf.shape
@@ -158,8 +158,35 @@
 
     def far_first(step):
         z = me // GROUP
-        upper = lax.rem(z // half + 1 + step // half, 2)
-        return upper * half + lax.rem(z + 1 + step, half)
+        upper = z // half
+        across = 1 - step // half
+        far = lax.rem(step, half)
+        near = lax.rem(z + 1 + step, half)
+        low = jnp.where(across == 1, far, near)
+        high = jnp.where(across == 1, half - 1 - far, near)
+        target = lax.rem(upper + across, 2)
+        return target * half + jnp.where(target == 0, low, high)
+
+    levels = n // GROUP
+    level = me // GROUP
+    pos = lax.rem(me, GROUP)
+    has_above = level + 1 < levels
+    has_below = level > 0
+    barrier = pltpu.get_barrier_semaphore()
+
+    def tell(sem, device):
+        pl.semaphore_signal(sem, inc=1, device_id={"seq": device}, device_id_type=MESH)
+
+    for k in range(1, GROUP):
+        tell(barrier, level * GROUP + lax.rem(pos + k, GROUP))
+
+    @pl.when(has_above)
+    def _():
+        tell(barrier, me + GROUP)
+
+    @pl.when(has_below)
+    def _():
+        tell(barrier, me - GROUP)
 
     cache_copy = pltpu.make_async_copy(c_ref, cbuf, c_sem)
     cache_copy.start()
@@ -170,14 +197,6 @@
     ]
     for copy in small:
         copy.start()
-    barrier = pltpu.get_barrier_semaphore()
-
-    def greet(k, _):
-        pl.semaphore_signal(barrier, inc=1, device_id={"seq": lax.rem(me + k, n)}, device_id_type=MESH)
-        return 0
-
-    lax.fori_loop(1, n, greet, 0)
-
     def own_q(h):
         return pltpu.make_async_copy(
             q_ref.at[:, pl.ds(pl.multiple_of((me * heads + h) * hd, hd), hd)],
@@ -192,25 +211,60 @@
     own_kv.start()
     for h in range(heads):
         own_q(h).start()
-    pl.semaphore_wait(barrier, n - 1)
-
-    def send_kv(k, _):
-        chip = lax.rem(my_chip + chips // 2 + k, chips)
-
-        @pl.when(chip != my_chip)
+    pl.semaphore_wait(barrier, GROUP - 1 + has_above.astype(jnp.int32) + has_below.astype(jnp.int32))
+
+    def send_kv(chip):
+        pltpu.make_async_remote_copy(
+            src_ref=kv_ref.at[:, kv_cols(chip)],
+            dst_ref=kvbuf.at[my_chip, core],
+            send_sem=kv_send,
+            recv_sem=kv_recv,
+            device_id={"seq": 2 * chip + core},
+            device_id_type=MESH,
+        ).start()
+
+    pairs = GROUP // 2
+
+    def kv_to_level(at, first):
+        for k in range(first, pairs):
+            send_kv(at * pairs + lax.rem(pos // 2 + k, pairs))
+
+    @pl.when(has_above)
+    def _():
+        tell(below_sem, me + GROUP)
+        send_kv(my_chip + pairs)
+
+    @pl.when(has_below)
+    def _():
+        tell(above_sem, me - GROUP)
+        send_kv(my_chip - pairs)
+
+    def learn(k, first):
+        @pl.when(level + k < levels)
         def _():
-            pltpu.make_async_remote_copy(
-                src_ref=kv_ref.at[:, kv_cols(chip)],
-                dst_ref=kvbuf.at[my_chip, core],
-                send_sem=kv_send,
-                recv_sem=kv_recv,
-                device_id={"seq": 2 * chip + core},
-                device_id_type=MESH,
-            ).start()
-
-        return 0
-
-    lax.fori_loop(0, chips, send_kv, 0)
+            pl.semaphore_wait(above_sem, 1)
+
+            @pl.when(has_below)
+            def _():
+                tell(above_sem, me - GROUP)
+
+            kv_to_level(level + k, first)
+
+        @pl.when(level >= k)
+        def _():
+            pl.semaphore_wait(below_sem, 1)
+
+            @pl.when(has_above)
+            def _():
+                tell(below_sem, me + GROUP)
+
+            kv_to_level(level - k, first)
+
+        return 0
+
+    learn(1, 1)
+    lax.fori_loop(2, levels, lambda k, _: learn(k, 0), 0)
+    kv_to_level(level, 1)
 
     def send_q(step, _):
         h = step // n
@@ -322,6 +376,7 @@
             pltpu.VMEM((rows, slots * TILE + reach * rows), f32),
             pltpu.VMEM((rows, TILE), f32),
             pltpu.VMEM((rows, 2 * hd), f32),
+            pltpu.SemaphoreType.REGULAR, pltpu.SemaphoreType.REGULAR,
             dma((3,)), dma, dma((heads + 2,)), dma, dma, dma, dma, dma, dma((heads,)), dma, dma,
         ],
         compiler_params=pltpu.CompilerParams(

time: 109 us -> 107 us (0.982)
  Pallas kernels: 108 us -> 105 us
    pallas_call x1, Pallas kernels: 108 us -> 105 us  [per_device(): pl.pallas_call(functools.partial(fused, n, kv_heads, slots), out_shape=pl...]
where the time goes in v1:
time: 107 us; the launch traced here: 106 us
  Pallas kernels  105 us (98%)
  local copies, waits for them, and re-layouts  1.32 us (1%)
    pallas_call x1, Pallas kernels, per_device(): pl.pallas_call(functools.partial(fused, n, kv_heads, slots), out_shape=pl...  105 us

profile of v1, /device:TPU:5, one launch (start us, length us, event | category | flops | bytes accessed | tf_op | source)
XLA Modules:
  0.0 106.1 jit_solution(1896935100175500401)
XLA Ops:
  0.0 104.8 %shard_map.64 = bf16[128,8192]{1,0:T(8,128)(2,1)S(1)} custom-call(s32[4,8,16]{2,1,0:T(8,128)} %bitcast.3, s32[4,16]{1,0:T(4,128)} %counts_ref.1, s32[16,16]{1,0:T(8,128)} %mask_ref.1, bf16[128,8192]{1,0:T(8,128)(2,1)} %q_ref.1, bf16[128,2048]{1,0:T(8,128)(2,1)} %kv_ref.1, bf16[64,128,256]{2,1,0:T(8,128)(2,1)} %bitcast.2), custom_call_target="tpu_custom_call" | custom-call | tf_op jit(solution)/shard_map/pallas_call | solution.py:363
  104.8 1.3 %copy.8 = bf16[128,8192]{1,0:T(8,128)(2,1)} copy(bf16[128,8192]{1,0:T(8,128)(2,1)S(1)} %shard_map.64) | data formatting | bytes 4194304

commit v2 on v1

--- a/solution.py
+++ b/solution.py
@@ -23,7 +23,9 @@
     return jnp.where(jnp.full(part.shape, value, jnp.int32) > above, part, NEG)
 
 
-def attend_block(h, b, slots, qbuf, kvbuf, cbuf, lists, counts, mask, scores, peaks, accum, obuf):
+def attend_block(
+    h, b, slots, qbuf, kvbuf, cbuf, lists, counts, mask, scores, peaks, accum, obuf, stats=None, half=0
+):
     hd = qbuf.shape[-1]
     rows = GROUP * TILE
     scale = math.log2(math.e) / math.sqrt(hd)
@@ -81,8 +83,9 @@
         span_scores(kb, False)
         return 0
 
-    lax.fori_loop(first, b, off_diagonal, 0)
-    span_scores(b, True)
+    lax.fori_loop(first, b if stats is None else half // GROUP, off_diagonal, 0)
+    if stats is None:
+        span_scores(b, True)
 
     def cache_mix(t, _):
         tile = b * GROUP + t
@@ -136,8 +139,67 @@
             accum[here, :] += jnp.dot(weights, values, preferred_element_type=jnp.float32)
         return 0
 
-    lax.fori_loop(first, b + 1, span_mix, 0)
+    lax.fori_loop(first, b + 1 if stats is None else half // GROUP, span_mix, 0)
+    if stats is not None:
+        for t in range(GROUP):
+            here = slice(t * TILE, (t + 1) * TILE)
+            level_of = peaks[here, :] * scale + jnp.log(accum[here, hd:]) * math.log2(math.e)
+            stats[h, b * GROUP + t - half] = jnp.transpose(level_of)[:1, :]
     obuf[h, pl.ds(base, rows), :] = (accum[:, :hd] / accum[:, hd:]).astype(jnp.bfloat16)
+
+
+def attend_local(i, pos, me, tiles, qloc, kvloc, mask, scores, peaks, accum, o_near, l_near):
+    hd = o_near.shape[-1]
+    scale = math.log2(math.e) / math.sqrt(hd)
+    at = pl.multiple_of(i // 2 * 2 * hd, 2 * hd)
+    q = jnp.concatenate(
+        [qloc[:, pl.ds(pl.multiple_of((i * GROUP + k) * hd, hd), hd)] for k in range(GROUP)], axis=0
+    )
+    peaks[...] = jnp.full(peaks.shape, NEG, jnp.float32)
+
+    def score(u, diagonal):
+        s = dot_t(q, kvloc[u // 2, u % 2, :, pl.ds(at, hd)])
+        s = keep_if(mask[me, tiles // 2 + u], 0, s)
+        if diagonal:
+            lower = lax.broadcasted_iota(jnp.int32, (TILE, TILE), 1) <= lax.broadcasted_iota(
+                jnp.int32, (TILE, TILE), 0
+            )
+            s = jnp.concatenate(
+                [jnp.where(lower, s[k * TILE : (k + 1) * TILE], NEG) for k in range(GROUP)], axis=0
+            )
+        scores[:, pl.ds(pl.multiple_of(u * TILE, TILE), TILE)] = s
+        peaks[...] = jnp.maximum(peaks[...], s)
+
+    def earlier(u, _):
+        score(u, False)
+        return 0
+
+    lax.fori_loop(0, pos, earlier, 0)
+    score(pos, True)
+    peak = jnp.max(peaks[...], axis=1, keepdims=True)
+    peaks[...] = jnp.broadcast_to(peak, peaks.shape)
+    accum[...] = jnp.zeros(accum.shape, jnp.float32)
+
+    def mix(u, _):
+        values = jnp.concatenate(
+            [
+                kvloc[u // 2, u % 2, :, pl.ds(pl.multiple_of(at + hd, hd), hd)],
+                jnp.ones((TILE, hd), jnp.bfloat16),
+            ],
+            axis=1,
+        )
+        weights = jnp.exp2(
+            (scores[:, pl.ds(pl.multiple_of(u * TILE, TILE), TILE)] - peaks[...]) * scale
+        ).astype(jnp.bfloat16)
+        accum[...] += jnp.dot(weights, values, preferred_element_type=jnp.float32)
+        return 0
+
+    lax.fori_loop(0, pos + 1, mix, 0)
+    for k in range(GROUP):
+        here = slice(k * TILE, (k + 1) * TILE)
+        total = accum[here, hd:]
+        o_near[i * GROUP + k] = accum[here, :hd] / total
+        l_near[i * GROUP + k] = peaks[here, :] * scale + jnp.log(total) * math.log2(math.e)
 
 
 def fused(
@@ -163,7 +225,7 @@
         far = lax.rem(step, half)
         near = lax.rem(z + 1 + step, half)
         low = jnp.where(across == 1, far, near)
-        high = jnp.where(across == 1, half - 1 - far, near)
+        high = near
         target = lax.rem(upper + across, 2)
         return target * half + jnp.where(target == 0, low, high)
 
@@ -213,6 +275,16 @@
         own_q(h).start()
     pl.semaphore_wait(barrier, GROUP - 1 + has_above.astype(jnp.int32) + has_below.astype(jnp.int32))
 
+    def q_to(peer, h):
+        pltpu.make_async_remote_copy(
+            src_ref=q_ref.at[:, pl.ds(pl.multiple_of((peer * heads + h) * hd, hd), hd)],
+            dst_ref=qbuf.at[h, pl.ds(pl.multiple_of(me * TILE, TILE), TILE), :],
+            send_sem=q_send,
+            recv_sem=q_recv.at[h],
+            device_id={"seq": peer},
+            device_id_type=MESH,
+        ).start()
+
     def send_kv(chip):
         pltpu.make_async_remote_copy(
             src_ref=kv_ref.at[:, kv_cols(chip)],
@@ -233,11 +305,15 @@
     def _():
         tell(below_sem, me + GROUP)
         send_kv(my_chip + pairs)
+        for h in range(heads):
+            q_to(me + GROUP, h)
 
     @pl.when(has_below)
     def _():
         tell(above_sem, me - GROUP)
         send_kv(my_chip - pairs)
+        for h in range(heads):
+            q_to(me - GROUP, h)
 
     def learn(k, first):
         @pl.when(level + k < levels)
@@ -271,16 +347,9 @@
         turn = lax.rem(step, n)
         peer = far_first(turn // GROUP) * GROUP + lax.rem(me + turn, GROUP)
 
-        @pl.when(peer != me)
+        @pl.when((peer != me) & (peer != me + GROUP) & (peer != me - GROUP))
         def _():
-            pltpu.make_async_remote_copy(
-                src_ref=q_ref.at[:, pl.ds(pl.multiple_of((peer * heads + h) * hd, hd), hd)],
-                dst_ref=qbuf.at[h, pl.ds(pl.multiple_of(me * TILE, TILE), TILE), :],
-                send_sem=q_send,
-                recv_sem=q_recv.at[h],
-                device_id={"seq": peer},
-                device_id_type=MESH,
-            ).start()
+            q_to(peer, h)
 
         return 0
 
@@ -349,6 +418,345 @@
     take(out_ref.at[:, pl.ds(0, heads * hd)], l_sem.at[heads + 1])
 
 
+def fused_split(
+    n, kv_heads, slots,
+    lists_ref, counts_ref, mask_ref, q_ref, kv_ref, c_ref, out_ref,
+    lists, counts, mask, qbuf, kvbuf, cbuf, obuf, scores, peaks, accum,
+    qloc, kvloc, o_near, l_near, stats, far_stats, far_o,
+    above_sem, below_sem, s_sem, c_sem, l_sem, kv_send, kv_recv, f_send, f_recv, q_send, q_recv, o_send, o_recv,
+    loc_send, loc_recv, lf_send, lf_recv, p_sem, ul_recv, st_send, st_recv, m_sem,
+):
+    me = lax.axis_index("seq")
+    heads, _, hd = qbuf.shape
+    chips = n // 2
+    core = lax.rem(me, 2)
+    sibling = me + 1 - 2 * core
+    my_chip = me // 2
+
+    blocks = n // GROUP
+    half = blocks // 2
+
+    def far_first(step, h):
+        z = me // GROUP
+        upper = z // half
+        across = 1 - step // half
+        far = lax.rem(step, half)
+        near = lax.rem(z + 1 + step, half)
+        low = jnp.where((across == 1) & (h >= 0), far, near)
+        high = jnp.where((across == 1) & (h == heads - 1), half - 1 - far, near)
+        target = lax.rem(upper + across, 2)
+        return target * half + jnp.where(target == 0, low, high)
+
+    levels = n // GROUP
+    level = me // GROUP
+    pos = lax.rem(me, GROUP)
+    has_above = level + 1 < levels
+    has_below = level > 0
+    barrier = pltpu.get_barrier_semaphore()
+
+    def tell(sem, device):
+        pl.semaphore_signal(sem, inc=1, device_id={"seq": device}, device_id_type=MESH)
+
+    for k in range(1, GROUP):
+        tell(barrier, level * GROUP + lax.rem(pos + k, GROUP))
+
+    @pl.when(has_above)
+    def _():
+        tell(barrier, me + GROUP)
+
+    @pl.when(has_below)
+    def _():
+        tell(barrier, me - GROUP)
+
+    cache_copy = pltpu.make_async_copy(c_ref, cbuf, c_sem)
+    cache_copy.start()
+
+    small = [
+        pltpu.make_async_copy(src, dst, s_sem.at[k])
+        for k, (src, dst) in enumerate(((lists_ref, lists), (counts_ref, counts), (mask_ref, mask)))
+    ]
+    for copy in small:
+        copy.start()
+    def own_q(h):
+        return pltpu.make_async_copy(
+            q_ref.at[:, pl.ds(pl.multiple_of((me * heads + h) * hd, hd), hd)],
+            qbuf.at[h, pl.ds(pl.multiple_of(me * TILE, TILE), TILE), :],
+            l_sem.at[h],
+        )
+
+    def kv_cols(chip):
+        return pl.ds(pl.multiple_of((2 * chip * kv_heads // n) * 2 * hd, 2 * hd), 2 * hd)
+
+    own_kv = pltpu.make_async_copy(kv_ref.at[:, kv_cols(my_chip)], kvbuf.at[my_chip, core], l_sem.at[heads])
+    own_kv.start()
+    near_n = n // 2
+    near_chips = chips // 2
+    low = me < near_n
+    high = me >= near_n
+    is_cut = my_chip == 0
+    loc_kv = kv_ref.at[:, pl.ds(0, 2 * hd)]
+    loc_slot = lax.rem(my_chip, near_chips)
+    own_loc_q = pltpu.make_async_copy(q_ref.at[:, pl.ds(0, 2 * heads * hd)], qloc, p_sem.at[0])
+    own_loc_kv = pltpu.make_async_copy(loc_kv, kvloc.at[loc_slot, core], p_sem.at[1])
+
+    @pl.when(high)
+    def _():
+        own_loc_q.start()
+        own_loc_kv.start()
+
+    for h in range(heads):
+        own_q(h).start()
+    pl.semaphore_wait(barrier, GROUP - 1 + has_above.astype(jnp.int32) + has_below.astype(jnp.int32))
+
+    def q_to(peer, h):
+        pltpu.make_async_remote_copy(
+            src_ref=q_ref.at[:, pl.ds(pl.multiple_of((peer * heads + h) * hd, hd), hd)],
+            dst_ref=qbuf.at[h, pl.ds(pl.multiple_of(me * TILE, TILE), TILE), :],
+            send_sem=q_send,
+            recv_sem=q_recv.at[h],
+            device_id={"seq": peer},
+            device_id_type=MESH,
+        ).start()
+
+    def send_kv(chip):
+        @pl.when(low | (chip > 0))
+        def _():
+            pltpu.make_async_remote_copy(
+                src_ref=kv_ref.at[:, kv_cols(chip)],
+                dst_ref=kvbuf.at[my_chip, core],
+                send_sem=kv_send,
+                recv_sem=kv_recv,
+                device_id={"seq": 2 * chip + core},
+                device_id_type=MESH,
+            ).start()
+
+    pairs = GROUP // 2
+
+    def kv_to_level(at, first):
+        for k in range(first, pairs):
+            send_kv(at * pairs + lax.rem(pos // 2 + k, pairs))
+
+    @pl.when(has_above)
+    def _():
+        tell(below_sem, me + GROUP)
+        send_kv(my_chip + pairs)
+        for h in range(heads):
+            q_to(me + GROUP, h)
+
+    @pl.when(has_below)
+    def _():
+        tell(above_sem, me - GROUP)
+        send_kv(my_chip - pairs)
+        for h in range(heads):
+            q_to(me - GROUP, h)
+
+    def learn(k, first):
+        @pl.when(level + k < levels)
+        def _():
+            pl.semaphore_wait(above_sem, 1)
+
+            @pl.when(has_below)
+            def _():
+                tell(above_sem, me - GROUP)
+
+            kv_to_level(level + k, first)
+
+        @pl.when(level >= k)
+        def _():
+            pl.semaphore_wait(below_sem, 1)
+
+            @pl.when(has_above)
+            def _():
+                tell(below_sem, me + GROUP)
+
+            kv_to_level(level - k, first)
+
+        return 0
+
+    learn(1, 1)
+    lax.fori_loop(2, levels, lambda k, _: learn(k, 0), 0)
+    kv_to_level(level, 1)
+
+    def send_q(step, _):
+        h = step // n
+        turn = lax.rem(step, n)
+        peer = far_first(turn // GROUP, h) * GROUP + lax.rem(me + turn, GROUP)
+
+        @pl.when((peer != me) & (peer != me + GROUP) & (peer != me - GROUP))
+        def _():
+            q_to(peer, h)
+
+        return 0
+
+    @pl.when(high)
+    def _():
+        for k in range(1, near_chips):
+            pltpu.make_async_remote_copy(
+                src_ref=loc_kv,
+                dst_ref=kvloc.at[loc_slot, core],
+                send_sem=loc_send,
+                recv_sem=loc_recv,
+                device_id={"seq": 2 * (near_chips + lax.rem(my_chip + k, near_chips)) + core},
+                device_id_type=MESH,
+            ).start()
+
+    lax.fori_loop(0, heads * n, send_q, 0)
+
+    def take(ref, sem):
+        pltpu.make_async_copy(ref, ref, sem).wait()
+
+    def to_sibling(ref, send, recv):
+        return pltpu.make_async_remote_copy(
+            src_ref=ref,
+            dst_ref=ref,
+            send_sem=send,
+            recv_sem=recv,
+            device_id={"seq": sibling},
+            device_id_type=MESH,
+        )
+
+    own_kv.wait()
+    cache_copy.wait()
+    for copy in small:
+        copy.wait()
+    forward_all = to_sibling(kvbuf.at[:, core], f_send, f_recv)
+    forward_low = to_sibling(kvbuf.at[pl.ds(0, near_chips), core], f_send, f_recv)
+    forward_loc = to_sibling(kvloc.at[:, core], lf_send, lf_recv)
+
+    @pl.when(is_cut)
+    def _():
+        take(kvbuf.at[pl.ds(0, near_chips - 1), 0], kv_recv)
+        forward_low.start()
+        forward_low.wait()
+
+    @pl.when(jnp.logical_not(is_cut))
+    def _():
+        take(kvbuf.at[pl.ds(0, chips - 1), 0], kv_recv)
+        forward_all.start()
+        forward_all.wait()
+
+    @pl.when(high)
+    def _():
+        own_loc_q.wait()
+        own_loc_kv.wait()
+        take(kvloc.at[pl.ds(0, near_chips - 1), 0], loc_recv)
+        forward_loc.start()
+
+    def local(i, _):
+        attend_local(i, me - near_n, me, n, qloc, kvloc, mask, scores, peaks, accum, o_near, l_near)
+        return 0
+
+    def one_head(h, _):
+        @pl.when(high & (h == 1))
+        def _():
+            forward_loc.wait()
+            lax.fori_loop(0, 2, local, 0)
+
+        own_q(h).wait()
+        take(qbuf.at[h, pl.ds(0, (n - 1) * TILE), :], q_recv.at[h])
+
+        def one_block(step, _):
+            b = far_first(step, h)
+            partial = is_cut & (b >= half)
+
+            @pl.when(partial)
+            def _():
+                attend_block(
+                    h, b, slots, qbuf, kvbuf, cbuf, lists, counts, mask, scores, peaks, accum, obuf,
+                    stats, near_n,
+                )
+                for t in range(GROUP):
+                    peer = b * GROUP + t
+                    for src, dst, send, recv in (
+                        (obuf.at[h, pl.ds(pl.multiple_of(peer * TILE, TILE), TILE), :], far_o.at[h, core], o_send, ul_recv),
+                        (stats.at[h, peer - near_n], far_stats.at[h, core], st_send, st_recv),
+                    ):
+                        pltpu.make_async_remote_copy(
+                            src_ref=src,
+                            dst_ref=dst,
+                            send_sem=send,
+                            recv_sem=recv.at[h],
+                            device_id={"seq": peer},
+                            device_id_type=MESH,
+                        ).start()
+
+            @pl.when(jnp.logical_not(partial))
+            def _():
+                attend_block(
+                    h, b, slots, qbuf, kvbuf, cbuf, lists, counts, mask, scores, peaks, accum, obuf
+                )
+                cols = pl.ds(pl.multiple_of((me * heads + h) * hd, hd), hd)
+                for t in range(GROUP):
+                    peer = b * GROUP + t
+                    src = obuf.at[h, pl.ds(pl.multiple_of(peer * TILE, TILE), TILE), :]
+
+                    @pl.when(peer != me)
+                    def _():
+                        pltpu.make_async_remote_copy(
+                            src_ref=src,
+                            dst_ref=out_ref.at[:, cols],
+                            send_sem=o_send,
+                            recv_sem=o_recv,
+                            device_id={"seq": peer},
+                            device_id_type=MESH,
+                        ).start()
+
+                    @pl.when(peer == me)
+                    def _():
+                        pltpu.make_async_copy(src, out_ref.at[:, cols], l_sem.at[heads + 1]).start()
+
+            return 0
+
+        lax.fori_loop(0, blocks, one_block, 0)
+        return 0
+
+    lax.fori_loop(0, heads, one_head, 0)
+
+    def tile_cols(count):
+        return q_ref.at[:, pl.ds(0, count * hd)]
+
+    @pl.when(high)
+    def _():
+        def merge_head(h, _):
+            take(far_o.at[h], ul_recv.at[h])
+            take(far_stats.at[h], st_recv.at[h])
+
+            def merge(owner, _):
+                i = owner * heads + h
+                cols = pl.ds(pl.multiple_of(i * hd, hd), hd)
+                l_far = jnp.transpose(jnp.broadcast_to(far_stats[h, owner], (TILE, TILE)))
+                l_own = l_near[i]
+                top = jnp.maximum(l_far, l_own)
+                w_far = jnp.exp2(l_far - top)
+                w_own = jnp.exp2(l_own - top)
+                mixed = far_o[h, owner].astype(jnp.float32) * w_far + o_near[i] * w_own
+                far_o[h, owner] = (mixed / (w_far + w_own)).astype(jnp.bfloat16)
+                pltpu.make_async_copy(far_o.at[h, owner], out_ref.at[:, cols], m_sem).start()
+                return 0
+
+            lax.fori_loop(0, 2, merge, 0)
+            return 0
+
+        lax.fori_loop(0, heads, merge_head, 0)
+        take(kvbuf.at[pl.ds(0, chips - 2), 0], kv_send)
+        take(kvloc.at[pl.ds(0, near_chips - 1), 0], loc_send)
+        take(tile_cols((n - 3) * heads), o_recv)
+        take(far_o, m_sem)
+
+    @pl.when(low)
+    def _():
+        take(kvbuf.at[pl.ds(0, chips - 1), 0], kv_send)
+        take(tile_cols((n - 1) * heads), o_recv)
+
+    @pl.when(is_cut)
+    def _():
+        take(stats, st_send)
+
+    take(tile_cols((n - 1) * heads), q_send)
+    take(tile_cols((n - 1) * heads), o_send)
+    take(out_ref.at[:, pl.ds(0, heads * hd)], l_sem.at[heads + 1])
+
+
 def per_device(queries, new_kv, cache, tile_lists, tile_counts, tile_mask):
     n = lax.axis_size("seq")
     hd = cache.shape[2] // 2
@@ -360,6 +768,43 @@
     bf, f32 = jnp.bfloat16, jnp.float32
     dma = pltpu.SemaphoreType.DMA
     hbm = pl.BlockSpec(memory_space=pl.ANY)
+    lists_of = tile_lists.transpose(0, 2, 1)
+    levels = n // GROUP
+    operands = lists_of, tile_counts, tile_mask, queries, new_kv, cache.reshape(-1, TILE, 2 * hd)
+    if levels % 2 == 0 and levels <= REACH + 1 and 2 * kv_heads == n and heads == GROUP and n == tiles:
+        near = n // 2
+        vm, sm = pltpu.VMEM, pltpu.SMEM
+        return pl.pallas_call(
+            functools.partial(fused_split, n, kv_heads, slots),
+            out_shape=vm(queries.shape, bf),
+            in_specs=[hbm] * 6,
+            out_specs=hbm,
+            scratch_shapes=[
+                sm((heads, slots, tiles), jnp.int32),
+                sm((heads, tiles), jnp.int32),
+                sm(tile_mask.shape, jnp.int32),
+                vm((heads, tokens, hd), bf),
+                vm((n // 2, 2, TILE, 2 * hd), bf),
+                vm((cache.shape[1] // TILE, TILE, 2 * hd), bf),
+                vm((heads, tokens, hd), bf),
+                vm((rows, slots * TILE + reach * rows), f32),
+                vm((rows, TILE), f32),
+                vm((rows, 2 * hd), f32),
+                vm((TILE, 2 * heads * hd), bf),
+                vm((near // 2, 2, TILE, 2 * hd), bf),
+                vm((2 * heads, TILE, hd), f32),
+                vm((2 * heads, TILE, hd), f32),
+                vm((heads, near, 1, TILE), f32),
+                vm((heads, 2, 1, TILE), f32),
+                vm((heads, 2, TILE, hd), bf),
+                pltpu.SemaphoreType.REGULAR, pltpu.SemaphoreType.REGULAR,
+                dma((3,)), dma, dma((heads + 2,)), dma, dma, dma, dma, dma, dma((heads,)), dma, dma,
+                dma, dma, dma, dma, dma((2,)), dma((heads,)), dma, dma((heads,)), dma,
+            ],
+            compiler_params=pltpu.CompilerParams(
+                collective_id=0, has_side_effects=True, vmem_limit_bytes=60 * 1024 * 1024
+            ),
+        )(*operands)
     return pl.pallas_call(
         functools.partial(fused, n, kv_heads, slots),
         out_shape=pltpu.VMEM(queries.shape, bf),
@@ -382,7 +827,7 @@
         compiler_params=pltpu.CompilerParams(
             collective_id=0, has_side_effects=True, vmem_limit_bytes=60 * 1024 * 1024
         ),
-    )(tile_lists.transpose(0, 2, 1), tile_counts, tile_mask, queries, new_kv, cache.reshape(-1, TILE, 2 * hd))
+    )(*operands)
 
 
 def solution(mesh):

time: 107 us -> 107 us (level)
  the two profiles are of different devices: /device:TPU:5 before, /device:TPU:21 now
where the time goes in v2:
time: 107 us; the launch traced here: 106 us
  Pallas kernels  105 us (98%)
  local copies, waits for them, and re-layouts  1.32 us (1%)
    pallas_call x1, Pallas kernels, per_device(): pl.pallas_call(functools.partial(fused_split, n, kv_heads, slots), out_sh...  105 us

profile of v2, /device:TPU:21, one launch (start us, length us, event | category | flops | bytes accessed | tf_op | source)
XLA Modules:
  0.0 106.4 jit_solution(17861555262408804638)
XLA Ops:
  0.0 105.0 %shard_map.64 = bf16[128,8192]{1,0:T(8,128)(2,1)S(1)} custom-call(s32[4,8,16]{2,1,0:T(8,128)} %bitcast.3, s32[4,16]{1,0:T(4,128)} %counts_ref.1, s32[16,16]{1,0:T(8,128)} %mask_ref.1, bf16[128,8192]{1,0:T(8,128)(2,1)} %q_ref.1, bf16[128,2048]{1,0:T(8,128)(2,1)} %kv_ref.1, bf16[64,128,256]{2,1,0:T(8,128)(2,1)} %bitcast.2), custom_call_target="tpu_custom_call" | custom-call | tf_op jit(solution)/shard_map/pallas_call | solution.py:777
  105.1 1.3 %copy.8 = bf16[128,8192]{1,0:T(8,128)(2,1)} copy(bf16[128,8192]{1,0:T(8,128)(2,1)S(1)} %shard_map.64) | data formatting | bytes 4194304
